TPU v7x, 256 devices: a whole 4x4x8 slice. The times are simulated.
256 devices in a mesh: grp: 8 (over z_lo, core), slab: 32 (over z_hi, x, y).
Axes of the slice: x: 4, y: 4, z: 8 (z_hi: 2, z_lo: 4; z = z_hi * 4 + z_lo), core: 2. Of those that a mesh axis runs over, the one named last changes fastest.
Arguments:
- occ_orbitals: bfloat16 [1024, 64, 4096], P(('grp', 'slab')), may hold values from -6 to 6
- vir_orbitals: bfloat16 [2048, 64, 4096], P(('grp', 'slab')), may hold values from -6 to 6
- pair_occ: int32 [8192], P(('grp', 'slab')), may hold values from 0 to 3
- pair_vir: int32 [8192], P(('grp', 'slab')), may hold values from 0 to 7
- sketch: bfloat16 [8192, 1024], P('grp'), may hold values from -6 to 6
Outputs:
- vertex: float32 [8192, 1024], P(('grp', 'slab'))
Inputs may be any that keep to these rules, and one draw needn't show every extreme that they name: `pair_occ`: an index into the 4 occupied orbitals held by the same device as the pair. `pair_vir`: an index into the 8 virtual orbitals held by the same device as the pair.
All inputs are finite; a program needn't handle non-finite values.
Results may differ from a plain program's by a relative error of at most 0.0057.
Values may be sent and summed in bfloat16 or wider, within the bound.
No kernel may reach another device: no remote copies, remote signals or barrier semaphores. Data moves between devices by JAX's collectives and lax.ppermute only.
A program may use at most 192 MiB of HBM per device.

v0:
```python
import math

import jax
import jax.numpy as jnp
from jax import lax
from jax.sharding import PartitionSpec as P

KYZ = 32


box_length = 10.0
screening = 1.0
epsilon = 1e-06


def real_basis(points, mode_count):
    grid_cells = jnp.arange(points, dtype=jnp.float32)[:, None]
    mode_index = jnp.arange(mode_count, dtype=jnp.int32)[None, :]
    frequency = (mode_index + 1) // 2
    phases = 2.0 * math.pi * grid_cells * frequency.astype(jnp.float32) / points
    values = jnp.where((mode_index % 2 == 1) | (mode_index == 0), jnp.cos(phases), jnp.sin(phases))
    factor = jnp.where(
        (mode_index == 0) | (2 * frequency == points),
        math.sqrt(1.0 / points),
        math.sqrt(2.0 / points),
    )
    return (values * factor).astype(jnp.bfloat16)


def coulomb_weight(modes_x, plane_count):
    freq_x = ((jnp.arange(modes_x, dtype=jnp.int32) + 1) // 2).astype(jnp.float32)
    freq_p = ((jnp.arange(plane_count, dtype=jnp.int32) + 1) // 2).astype(jnp.float32)
    plane_sq = (freq_p[:, None] * freq_p[:, None] + freq_p[None, :] * freq_p[None, :]).reshape(-1)
    summed_sq = plane_sq[:, None, None] + (freq_x * freq_x)[None, None, :]
    wave_sq = (2.0 * math.pi / box_length) ** 2 * summed_sq
    return jnp.sqrt(4.0 * math.pi / (wave_sq + screening * screening))


def pair_coefficients(occ_rows, vir_rows):
    pairs_dev = occ_rows.shape[0]
    grid_size = occ_rows.shape[1]
    basis_x = real_basis(grid_size, grid_size)
    basis_plane = real_basis(grid_size, KYZ)
    density = (occ_rows.astype(jnp.float32) * vir_rows.astype(jnp.float32)).astype(jnp.bfloat16)
    along_x = jnp.einsum(
        "pxs,xk->pks", density, basis_x, preferred_element_type=jnp.float32
    ).astype(jnp.bfloat16)
    planes = along_x.reshape(pairs_dev * grid_size, grid_size, grid_size)
    second = jnp.einsum(
        "ayz,zc->cya", planes, basis_plane, preferred_element_type=jnp.float32
    ).astype(jnp.bfloat16)
    along_y = jnp.einsum("cya,yb->bca", second, basis_plane, preferred_element_type=jnp.float32)
    weighted = along_y.reshape(KYZ * KYZ, pairs_dev, grid_size) * coulomb_weight(grid_size, KYZ)
    return weighted.astype(jnp.bfloat16)


def body(occ_orbitals, vir_orbitals, pair_occ, pair_vir, sketch):
    coulomb_rows = pair_coefficients(occ_orbitals[pair_occ], vir_orbitals[pair_vir])
    plane_modes, pairs_dev, modes_x = coulomb_rows.shape
    slab_count = lax.axis_size("slab")
    fields = sketch.shape[1]
    parcel = coulomb_rows.reshape(slab_count, plane_modes // slab_count, pairs_dev * modes_x)
    received = lax.all_to_all(parcel, "slab", split_axis=0, concat_axis=2, tiled=True)
    item_count = received.shape[1]
    grouped = received[0].reshape(item_count, -1, modes_x)
    partial_value = jnp.einsum("npk,pf->nkf", grouped, sketch, preferred_element_type=jnp.float32)
    partial_value, local_rows = (partial_value, received[0])
    flattened = partial_value.reshape(-1, fields)
    coef_count = plane_modes * modes_x
    portion = lax.psum_scatter(flattened, "grp", scatter_dimension=1, tiled=True)
    squares = lax.psum(jnp.sum(portion * portion, axis=0), "slab")
    scaled = (portion * lax.rsqrt(squares / coef_count + epsilon)).astype(jnp.bfloat16)
    field_basis = lax.all_gather(scaled, "grp", axis=1, tiled=True)
    slab_modes = field_basis.shape[0] // modes_x
    basis_rows = field_basis.reshape(slab_modes, modes_x, fields)
    gamma_rows = local_rows.reshape(slab_modes, -1, modes_x)
    summed = lax.psum_scatter(
        jnp.einsum("ypk,ykf->pf", gamma_rows, basis_rows, preferred_element_type=jnp.float32),
        "slab",
        scatter_dimension=0,
        tiled=True,
    )
    return summed * (1.0 / math.sqrt(coef_count))


def solution(mesh):
    return jax.shard_map(
        body,
        mesh=mesh,
        in_specs=(
            P(("grp", "slab"), None, None),
            P(("grp", "slab"), None, None),
            P(("grp", "slab")),
            P(("grp", "slab")),
            P("grp", None),
        ),
        out_specs=P(("grp", "slab"), None),
        check_vma=False,
    )
```

profile of v0, /device:TPU:32, one launch (start us, length us, event | category | flops | bytes accessed | tf_op | source)
XLA Modules:
  0.0 870.2 jit_solution(2158189540496240035)
XLA Ops:
  6.5 0.0 copy-start
  6.5 0.0 reduce-scatter.3.cloned.1.call-start
  6.6 0.8 compare_select_fusion.1
  7.4 0.7 compare_select_fusion
  8.1 0.0 copy-done
  8.1 7.2 gather_fusion
  15.3 9.4 %gather_fusion.1 = bf16[32,64,4096]{2,1,0:T(8,128)(2,1)} fusion(bf16[8,64,4096]{2,1,0:T(8,128)(2,1)} %param.6, s32[1024]{0:T(1024)S(1)} %pad_clamp_fusion), kind=kCustom, calls=%fused_computation.1 | custom fusion | bytes 33554560 | tf_op jit(solution)/shard_map/gather | solution.py:58
  24.7 23.4 %convert_bitcast_fusion = bf16[32,64,4096]{2,1,0:T(8,128)(2,1)} fusion(bf16[32,64,4096]{2,1,0:T(8,128)(2,1)} %gather_fusion.1, bf16[32,64,4096]{2,1,0:T(8,128)(2,1)} %gather_fusion, f32[64]{0:T(128)S(1)} %get-tuple-element.5, f32[64]{0:T(128)S(1)} %fusion.20, f32[64]{0:T(128)S(1)} %get-tuple-element.6, pred[64]{0:T(512)(128)(4,1)S(1)} %compare_or_fusion), kind=kOutput, calls=%fused_computation.6 | convolution fusion | flops 1115705344 | bytes 50332480 | tf_op jit(solution)/shard_map/pxs,xk->pks/dot_general | solution.py:45
  48.2 46.0 %reshape.261 = bf16[2048,64,64]{2,1,0:T(8,128)(2,1)} reshape(bf16[32,64,4096]{2,1,0:T(8,128)(2,1)} %convert_bitcast_fusion) | data formatting | bytes 33554432 | tf_op jit(solution)/shard_map/reshape | solution.py:48
  94.2 0.1 broadcast_add_fusion
  94.2 0.1 add.182
  94.3 0.2 divide_sqrt_fusion
  94.5 0.2 copy.19
  94.7 6.8 mul.166
  101.5 14.8 %mul.167 = f32[32,32,2048]{2,1,0:T(8,128)} reshape(f32[1024,32,64]{2,1,0:T(8,128)} %mul.166) | data formatting | bytes 16777216 | tf_op jit(solution)/shard_map/mul | solution.py:53
  116.3 0.0 copy-start.2
  116.3 75.2 %convert_bitcast_fusion.1 = bf16[32,64,2048]{2,0,1:T(8,128)(2,1)} fusion(bf16[2048,64,64]{2,1,0:T(8,128)(2,1)} %reshape.261, f32[32]{0:T(128)S(1)} %or_select_fusion.1, f32[32]{0:T(128)S(1)} %fusion.21, f32[64]{0:T(128)S(1)} %get-tuple-element.6, pred[32]{0:T(512)(128)(4,1)S(1)} %compare_or_fusion.1), kind=kOutput, calls=%fused_computation.11 | convolution fusion | flops 541075456 | bytes 25166368 | tf_op jit(solution)/shard_map/ayz,zc->cya/dot_general | solution.py:49
  191.5 0.0 copy-done.2
  191.5 18.1 %fusion.3 = bf16[32,32,2048]{2,0,1:T(8,128)(2,1)S(1)} fusion(f32[32,32,2048]{2,1,0:T(8,128)S(1)} %copy-done.2, bf16[32,64,2048]{2,0,1:T(8,128)(2,1)} %convert_bitcast_fusion.1, f32[32]{0:T(128)S(1)} %or_select_fusion.1, f32[32]{0:T(128)S(1)} %fusion.21, f32[64]{0:T(128)S(1)} %get-tuple-element.6, pred[32]{0:T(512)(128)(4,1)S(1)} %compare_or_fusion.1), kind=kOutput, calls=%fused_computation.8 | convolution fusion | flops 272640000 | bytes 20972064 | tf_op jit(solution)/shard_map/cya,yb->bca/dot_general | solution.py:52
  209.7 2.3 copy.21
  212.0 111.4 %all_to_all.15 = bf16[32,32,2048]{2,1,0:T(8,128)(2,1)S(1)} all-to-all(bf16[32,32,2048]{2,1,0:T(8,128)(2,1)S(1)} %copy.21), channel_id=1, replica_groups=mesh['grp'=8,'slab'=32] {'slab'}, dimensions={0} | all-to-all | bytes 8388608 | tf_op jit(solution)/shard_map/all_to_all | solution.py:63
  323.4 4.3 copy.22
  327.6 12.9 %reshape_squeeze.4 = bf16[32,1024,64]{2,1,0:T(8,128)(2,1)} reshape(bf16[1,32,32,2048]{3,2,1,0:T(8,128)(2,1)} %copy.22) | data formatting | bytes 8388608 | tf_op jit(solution)/shard_map/reshape;squeeze | solution.py:76
  340.5 0.0 copy-start.3
  340.5 8.7 copy.23
  349.2 0.0 copy-done.3
  349.2 8.9 %fusion.27 = f32[2048,1024]{1,0:T(8,128)} fusion(bf16[2048,1024]{1,0:T(8,128)(2,1)} %bitcast.27, bf16[1024,1024]{1,0:T(8,128)(2,1)S(1)} %copy-done.3), kind=kOutput, calls=%fused_computation.56 | convolution fusion | flops 4294967296 | bytes 14680064 | tf_op jit(solution)/shard_map/npk,pf->nkf/dot_general | solution.py:66
  358.1 0.0 reduce-scatter.3.cloned.1.call-update
  358.1 0.0 all-gather.2.cloned.1.call-start
  358.2 86.4 %reduce-scatter.3.cloned.1.call-done = f32[2048,128]{1,0:T(8,128)} async-done(((f32[2048,1024]{1,0:T(8,128)}), f32[2048,128]{1,0:T(8,128)}) %reduce-scatter.3.cloned.1.call-update) | async-done | bytes 1048592 | tf_op jit(solution)/shard_map/reduce_scatter | solution.py:70
  444.5 1.5 multiply_reduce_fusion
  446.0 118.9 %psum.7 = f32[128]{0:T(128)S(1)} all-reduce(f32[128]{0:T(128)S(1)} %multiply_reduce_fusion), channel_id=1, replica_groups=mesh['grp'=8,'slab'=32] {'slab'}, use_global_device_ids=true, to_apply=%region_2.3 | all-reduce | flops 128 | bytes 1024 | tf_op jit(solution)/shard_map/psum | solution.py:71
  564.9 2.1 multiply_convert_fusion.4
  567.0 0.0 all-gather.2.cloned.1.call-update
  567.0 0.0 reduce-scatter.5.cloned.1.call-start
  567.1 46.7 %all-gather.2.cloned.1.call-done = bf16[2048,1024]{1,0:T(8,128)(2,1)} async-done(((bf16[2048,128]{1,0:T(8,128)(2,1)}), bf16[2048,1024]{1,0:T(8,128)(2,1)}) %all-gather.2.cloned.1.call-update) | async-done | bytes 4194320 | tf_op jit(solution)/shard_map/all_gather | solution.py:73
  613.7 0.0 copy-start.1
  613.8 9.7 %convolution_bitcast_fusion = f32[1024,1024]{1,0:T(8,128)} fusion(bf16[32,1024,64]{2,1,0:T(8,128)(2,1)} %reshape_squeeze.4, bf16[32,64,1024]{2,1,0:T(8,128)(2,1)} %bitcast.28), kind=kOutput, calls=%fused_computation.12 | convolution fusion | flops 4294967296 | bytes 12582912 | tf_op jit(solution)/shard_map/ypk,ykf->pf/dot_general | solution.py:78
  623.4 0.0 reduce-scatter.5.cloned.1.call-update
  623.5 238.5 %reduce-scatter.5.cloned.1.call-done = f32[32,1024]{1,0:T(8,128)} async-done(((f32[1024,1024]{1,0:T(8,128)}), f32[32,1024]{1,0:T(8,128)}) %reduce-scatter.5.cloned.1.call-update) | async-done | bytes 131088 | tf_op jit(solution)/shard_map/reduce_scatter | solution.py:77
  861.9 1.6 broadcast_multiply_fusion
  863.5 0.0 copy-done.1
  (11 shorter events, 0.1 us)
Async XLA Ops:
  6.5 1.6 copy-start
  6.5 438.0 %reduce-scatter.3.cloned.1.call-start = ((), (), s32[]{:S(2)}) async-start(), calls=%async_computation.3 | async-start | bytes 9437184 | tf_op jit(solution)/shard_map/reduce_scatter | solution.py:70
  116.3 75.2 %copy-start.2 = (f32[32,32,2048]{2,1,0:T(8,128)S(1)}, f32[32,32,2048]{2,1,0:T(8,128)}, u32[]{:S(2)}) copy-start(f32[32,32,2048]{2,1,0:T(8,128)} %mul.167) | copy-start | bytes 25165828
  340.5 8.7 copy-start.3
  358.1 255.6 %all-gather.2.cloned.1.call-start = ((), (), s32[]{:S(2)}) async-start(), calls=%async_computation.4 | async-start | bytes 4718592 | tf_op jit(solution)/shard_map/all_gather | solution.py:73
  567.0 294.9 %reduce-scatter.5.cloned.1.call-start = ((), (), s32[]{:S(2)}) async-start(), calls=%async_computation.5 | async-start | bytes 4325376 | tf_op jit(solution)/shard_map/reduce_scatter | solution.py:77
  613.7 249.8 %copy-start.1 = (bf16[4,64,4096]{2,1,0:T(8,128)(2,1)S(1)}, bf16[4,64,4096]{2,1,0:T(8,128)(2,1)}, u32[]{:S(2)}) copy-start(bf16[4,64,4096]{2,1,0:T(8,128)(2,1)} %param.5) | copy-start | bytes 6291460
Sparse Core Ops, SparseCore 0:
  358.2 86.2 reduce-scatter.2
  567.1 46.5 all-gather.1
  623.6 238.3 reduce-scatter.4
where the time goes:
time: 878 us; the launch traced here: 870 us
  waiting for transfers between devices  372 us (42%)
  blocking collectives  230 us (26%)
  matrix products  135 us (15%)
  local copies, waits for them, and re-layouts  113 us (13%)
  between operations  13.4 us (2%)
    reduce_scatter x1, waiting for transfers between devices, body(): lax.psum_scatter(jnp.einsum('ypk,ykf->pf', gamma_rows, basis_rows, prefer...  238 us
    psum x1, blocking collectives, body(): squares = lax.psum(jnp.sum(portion * portion, axis=0), 'slab')  119 us
    all_to_all x1, blocking collectives, body(): lax.all_to_all(parcel, 'slab', split_axis=0, concat_axis=2, tiled=True)  111 us
    reduce_scatter x1, waiting for transfers between devices, body(): lax.psum_scatter(flattened, 'grp', scatter_dimension=1, tiled=True)  86.4 us
    dot_general x1, matrix products, pair_coefficients(): jnp.einsum('ayz,zc->cya', planes, basis_plane, preferred_element_type=jnp...  75.2 us
    all_gather x1, waiting for transfers between devices, body(): field_basis = lax.all_gather(scaled, 'grp', axis=1, tiled=True)  46.7 us
    reshape x1, local copies, waits for them, and re-layouts, pair_coefficients(): planes = along_x.reshape(pairs_dev * grid_size, grid_size, grid_size)  46 us
    dot_general x1, matrix products, pair_coefficients(): jnp.einsum('pxs,xk->pks', density, basis_x, preferred_element_type=jnp.fl...  23.4 us
  transfers between devices with their start and end apart: 3, of which 3 were waited for; matrix products, arithmetic and copies ran while one was open for 0% of the time, Pallas kernels for 0%

commit v1 on v0

v1 whole, which is shorter than its diff:
```python
import math

import jax
import jax.numpy as jnp
import numpy as np
from jax import lax
from jax.sharding import Mesh, PartitionSpec as P

GRID = 64
KYZ = 32
box_length = 10.0
screening = 1.0
epsilon = 1e-06
PLANE = ("core", "x", "y")
RING = ("z_hi", "z_lo")


def real_basis(points, mode_count):
    cell = np.arange(points, dtype=np.float32)[:, None]
    mode = np.arange(mode_count, dtype=np.int32)[None, :]
    freq = (mode + 1) // 2
    phases = 2.0 * math.pi * cell * freq.astype(np.float32) / points
    values = np.where((mode % 2 == 1) | (mode == 0), np.cos(phases), np.sin(phases))
    factor = np.where((mode == 0) | (2 * freq == points), math.sqrt(1.0 / points), math.sqrt(2.0 / points))
    return jnp.asarray((values * factor).astype(np.float32)).astype(jnp.bfloat16)


def coulomb_weight(modes_x, modes_p):
    freq_x = ((jnp.arange(modes_x, dtype=jnp.int32) + 1) // 2).astype(jnp.float32)
    freq_p = ((jnp.arange(modes_p, dtype=jnp.int32) + 1) // 2).astype(jnp.float32)
    plane_sq = (freq_p[:, None] * freq_p[:, None] + freq_p[None, :] * freq_p[None, :]).reshape(-1)
    summed_sq = (freq_x * freq_x)[:, None] + plane_sq[None, :]
    wave_sq = (2.0 * math.pi / box_length) ** 2 * summed_sq
    return jnp.sqrt(4.0 * math.pi / (wave_sq + screening * screening))


def body(occ_orbitals, vir_orbitals, pair_occ, pair_vir, sketch):
    pairs = pair_occ.shape[0]
    fields = sketch.shape[1]
    coef_count = GRID * KYZ * KYZ
    f32 = jnp.float32
    mine = sketch.reshape(2, -1, fields)[lax.axis_index("z_hi")]
    sketch_plane = lax.all_gather(mine, "core", axis=0, tiled=True)

    basis_x = real_basis(GRID, GRID)
    basis_p = real_basis(GRID, KYZ)
    density = (occ_orbitals[pair_occ] * vir_orbitals[pair_vir]).reshape(pairs * GRID, GRID * GRID)
    kron_yz = (basis_p.astype(f32)[:, None, :, None] * basis_p.astype(f32)[None, :, None, :]).reshape(
        GRID * GRID, KYZ * KYZ
    ).astype(jnp.bfloat16)
    second = jnp.dot(density, kron_yz, preferred_element_type=f32).astype(jnp.bfloat16)
    half = 16
    eye = jnp.eye(half, dtype=jnp.bfloat16)
    mix_x = (basis_x.T[:, None, None, :] * eye[None, :, :, None]).reshape(GRID * half, half * GRID)
    blocks = second.reshape(pairs // half, half * GRID, KYZ * KYZ)
    weight = coulomb_weight(GRID, KYZ)
    parts = []
    for h in range(pairs // half):
        along = jnp.dot(mix_x, blocks[h], preferred_element_type=f32).reshape(GRID, half, KYZ * KYZ)
        parts.append((along * weight[:, None, :]).astype(jnp.bfloat16))
    gamma = jnp.concatenate(parts, axis=1)

    slabs = gamma.reshape(32, 2, pairs, KYZ * KYZ)
    received, terms = [], []
    for h in range(2):
        got = lax.all_to_all(slabs[:, h], PLANE, split_axis=0, concat_axis=0, tiled=True)
        got = got.reshape(32 * pairs, KYZ * KYZ)
        received.append(got)
        part = lax.dot_general(sketch_plane, got, (((0,), (0,)), ((), ())), preferred_element_type=f32)
        part = part.astype(jnp.bfloat16)
        mine_sum = lax.psum_scatter(part, RING, scatter_dimension=0, tiled=True)
        whole = lax.all_gather(mine_sum, RING, axis=0, tiled=True)
        terms.append(whole)
    squares = sum(jnp.sum(jnp.square(t.astype(f32)), axis=1) for t in terms)
    vertex = sum(
        lax.dot_general(g, t, (((1,), (1,)), ((), ())), preferred_element_type=f32)
        for g, t in zip(received, terms)
    ).astype(jnp.bfloat16)
    all_squares = lax.all_gather(squares[None], PLANE, axis=0, tiled=True)
    scale = lax.rsqrt(jnp.sum(all_squares, axis=0) / coef_count + epsilon) * (1.0 / math.sqrt(coef_count))
    shares = lax.all_to_all(vertex.reshape(32, pairs, fields), PLANE, split_axis=0, concat_axis=0, tiled=True)
    return jnp.sum(shares.astype(f32), axis=0) * scale[None, :]


def solution(mesh):
    wide = Mesh(mesh.devices.reshape(4, 2, 2, 4, 4), ("z_lo", "core", "z_hi", "x", "y"))
    whole = ("z_lo", "core", "z_hi", "x", "y")
    return jax.shard_map(
        body,
        mesh=wide,
        in_specs=(P(whole), P(whole), P(whole), P(whole), P(("z_lo", "core"))),
        out_specs=P(whole),
        check_vma=False,
    )
```

time: 878 us -> 426 us (0.49)
  waiting for transfers between devices: 372 us -> 124 us
  matrix products: 135 us -> 50.5 us
  blocking collectives: 230 us -> 150 us
  local copies, waits for them, and re-layouts: 113 us -> 44.3 us
  other arithmetic: 6.96 us -> 32.5 us
    reduce_scatter x2, waiting for transfers between devices: 325 us -> 47.3 us  [body(): mine_sum = lax.psum_scatter(part, RING, scatter_dimension=0, tiled=True)]
    psum x1 -> x0, blocking collectives: 119 us -> none  [body(): squares = lax.psum(jnp.sum(portion * portion, axis=0), 'slab')]
    dot_general x5 -> x7, matrix products: 135 us -> 50.5 us  [the longest x1 23 us: body(): jnp.dot(density, kron_yz, preferred_element_type=f32).astype(jnp.bfloat16)]
    all_gather x0 -> x1, blocking collectives: none -> 82.5 us  [body(): all_squares = lax.all_gather(squares[None], PLANE, axis=0, tiled=True)]
    reshape x1 -> x0, local copies, waits for them, and re-layouts: 46 us -> none  [pair_coefficients(): planes = along_x.reshape(pairs_dev * grid_size, grid_size, grid_size)]
    all_to_all x1 -> x2, blocking collectives: 111 us -> 67.9 us  [body(): lax.all_to_all(slabs[:, h], PLANE, split_axis=0, concat_axis=0, tiled=True)]
    all_gather x1 -> x3, waiting for transfers between devices: 46.7 us -> 76.7 us  [the longest x2 76.7 us: body(): whole = lax.all_gather(mine_sum, RING, axis=0, tiled=True)]
    mul x2 -> x4, local copies, waits for them, and re-layouts: 21.6 us -> 0.45 us  [body(): basis_x.T[:, None, None, :] * eye[None, :, :, None]]
  transfers between devices with their start and end apart: 3 -> 6, of which waited for: 3 -> 4; matrix products, arithmetic and copies ran while one was open for 0% -> 25% of each run, Pallas kernels for 0% -> 0%
where the time goes in v1:
time: 426 us; the launch traced here: 423 us
  blocking collectives  150 us (35%)
  waiting for transfers between devices  124 us (29%)
  matrix products  50.5 us (12%)
  local copies, waits for them, and re-layouts  44.3 us (10%)
  other arithmetic  32.5 us (8%)
  between operations  13.4 us (3%)
  starting transfers between devices  7.65 us (2%)
    all_gather x1, blocking collectives, body(): all_squares = lax.all_gather(squares[None], PLANE, axis=0, tiled=True)  82.5 us
    all_gather x2, waiting for transfers between devices, body(): whole = lax.all_gather(mine_sum, RING, axis=0, tiled=True)  76.7 us
    all_to_all x2, blocking collectives, body(): lax.all_to_all(slabs[:, h], PLANE, split_axis=0, concat_axis=0, tiled=True)  67.9 us
    reduce_scatter x2, waiting for transfers between devices, body(): mine_sum = lax.psum_scatter(part, RING, scatter_dimension=0, tiled=True)  47.3 us
    dot_general x1, matrix products, body(): jnp.dot(density, kron_yz, preferred_element_type=f32).astype(jnp.bfloat16)  23 us
    convert_element_type x1, local copies, waits for them, and re-layouts, body(): kron_yz = (basis_p.astype(f32)[:, None, :, None] * basis_p.astype(f32)[No...  22.7 us
    mul x1, other arithmetic, body(): occ_orbitals[pair_occ] * vir_orbitals[pair_vir]  19.3 us
    dot_general x2, matrix products, body(): lax.dot_general(g, t, (((1,), (1,)), ((), ())), preferred_element_type=f32)  13.1 us
  transfers between devices with their start and end apart: 6, of which 4 were waited for; matrix products, arithmetic and copies ran while one was open for 25% of the time, Pallas kernels for 0%

profile of v1, /device:TPU:32, one launch (start us, length us, event | category | flops | bytes accessed | tf_op | source)
XLA Modules:
  0.0 422.8 jit_solution(1584889601855821825)
XLA Ops:
  6.5 0.0 all-gather.10.cloned.1.call-start
  6.6 2.4 constant_dynamic-slice_fusion
  9.0 0.0 all-gather.10.cloned.1.call-update
  9.0 0.0 reduce-scatter.3.cloned.1.call-start
  9.1 0.0 copy-done.8
  9.2 6.7 %multiply_convert_fusion = bf16[64,64,32,32]{1,0,3,2:T(8,128)(2,1)} fusion(f32[64,32]{0,1:T(8,128)S(1)} %copy-done.5), kind=kLoop, calls=%fused_computation.2 | loop fusion | flops 8388608 | bytes 8396800 | tf_op jit(solution)/shard_map/convert_element_type | solution.py:50
  15.9 22.7 %convert_element_type.83 = bf16[4096,1024]{0,1:T(8,128)(2,1)} reshape(bf16[64,64,32,32]{1,0,3,2:T(8,128)(2,1)} %multiply_convert_fusion) | data formatting | bytes 16777216 | tf_op jit(solution)/shard_map/convert_element_type | solution.py:50
  38.7 0.2 mul.133
  38.9 0.1 broadcast_add_fusion
  38.9 0.1 add.162
  39.0 0.1 mul.135
  39.1 0.1 mul.136
  39.2 0.0 copy-done
  39.3 7.2 %gather_fusion = bf16[32,64,4096]{2,1,0:T(8,128)(2,1)} fusion(bf16[4,64,4096]{2,1,0:T(8,128)(2,1)S(1)} %copy-done, s32[1024]{0:T(1024)S(1)} %pad_clamp_fusion.1), kind=kCustom, calls=%fused_computation | custom fusion | bytes 33554560 | tf_op jit(solution)/shard_map/gather | solution.py:47
  46.5 9.4 %gather_fusion.1 = bf16[32,64,4096]{2,1,0:T(8,128)(2,1)} fusion(bf16[8,64,4096]{2,1,0:T(8,128)(2,1)} %param.8, s32[1024]{0:T(1024)S(1)} %pad_clamp_fusion), kind=kCustom, calls=%fused_computation.1 | custom fusion | bytes 33554560 | tf_op jit(solution)/shard_map/gather | solution.py:47
  55.9 19.3 %mul.139 = bf16[32,64,4096]{2,1,0:T(8,128)(2,1)} multiply(bf16[32,64,4096]{2,1,0:T(8,128)(2,1)} %gather_fusion, bf16[32,64,4096]{2,1,0:T(8,128)(2,1)} %gather_fusion.1) | non-fusion elementwise | flops 8388608 | bytes 50331648 | tf_op jit(solution)/shard_map/mul | solution.py:47
  75.2 23.0 %convolution_convert_fusion = bf16[2048,1024]{1,0:T(8,128)(2,1)S(1)} fusion(bf16[2048,4096]{1,0:T(8,128)(2,1)} %bitcast.41, bf16[4096,1024]{0,1:T(8,128)(2,1)} %convert_element_type.83), kind=kOutput, calls=%fused_computation.10 | convolution fusion | flops 17181966336 | bytes 29360128 | tf_op jit(solution)/shard_map/dot_general | solution.py:51
  98.2 0.2 divide_sqrt_fusion
  98.3 2.3 multiply_convert_fusion.1
  100.7 2.3 multiply_convert_fusion.2
  103.0 0.8 pad_maximum_fusion
  103.9 0.6 slice_bitcast_fusion
  104.5 35.8 %all_to_all.15 = bf16[32,32,1024]{2,1,0:T(8,128)(2,1)} all-to-all(bf16[32,32,1024]{2,1,0:T(8,128)(2,1)S(1)} %get-tuple-element.6), channel_id=1, replica_groups=mesh['z_lo'=4,'core'=2,'z_hi'=2,'x'=4,'y'=4] {'core','x','y'}, dimensions={0} | all-to-all | bytes 4194304 | tf_op jit(solution)/shard_map/all_to_all | solution.py:66
  140.3 5.9 %fusion.8 = bf16[1024,1024]{1,0:T(8,128)(2,1)} fusion(bf16[1024,1024]{1,0:T(8,128)(2,1)} %bitcast.43, bf16[1,1024,1024]{2,1,0:T(8,128)(2,1)} %all-gather.10.cloned.1.call-done), kind=kOutput, calls=%fused_computation.23 | convolution fusion | flops 2148532224 | bytes 6291456 | tf_op jit(solution)/shard_map/dot_general | solution.py:69
  146.2 0.0 reduce-scatter.3.cloned.1.call-update
  146.2 0.0 reduce-scatter.5.cloned.1.call-start
  146.3 32.1 %all_to_all.16 = bf16[32,32,1024]{2,1,0:T(8,128)(2,1)S(1)} all-to-all(bf16[32,32,1024]{2,1,0:T(8,128)(2,1)S(1)} %get-tuple-element.5), channel_id=1, replica_groups=mesh['z_lo'=4,'core'=2,'z_hi'=2,'x'=4,'y'=4] {'core','x','y'}, dimensions={0} | all-to-all | bytes 4194304 | tf_op jit(solution)/shard_map/all_to_all | solution.py:66
  178.4 1.3 copy-done.3
  179.7 3.8 fusion.11
  183.5 0.0 reduce-scatter.5.cloned.1.call-update
  183.5 0.0 all-gather.6.cloned.1.call-start
  183.6 3.5 reduce-scatter.3.cloned.1.call-done
  187.1 0.0 all-gather.6.cloned.1.call-update
  187.1 0.3 all-gather.8.cloned.1.call-start
  187.4 43.8 %reduce-scatter.5.cloned.1.call-done = bf16[128,1024]{1,0:T(8,128)(2,1)} async-done(((bf16[1024,1024]{1,0:T(8,128)(2,1)}), bf16[128,1024]{1,0:T(8,128)(2,1)}) %reduce-scatter.5.cloned.1.call-update) | async-done | bytes 262160 | tf_op jit(solution)/shard_map/reduce_scatter | solution.py:71
  231.2 0.0 all-gather.8.cloned.1.call-update
  231.2 41.5 %all-gather.6.cloned.1.call-done = bf16[1024,1024]{1,0:T(8,128)(2,1)} async-done(((bf16[128,1024]{1,0:T(8,128)(2,1)}), bf16[1024,1024]{1,0:T(8,128)(2,1)}) %all-gather.6.cloned.1.call-update) | async-done | bytes 2097168 | tf_op jit(solution)/shard_map/all_gather | solution.py:72
  272.8 5.9 %fusion.23 = f32[1024,1024]{1,0:T(8,128)} fusion(bf16[1024,1024]{1,0:T(8,128)(2,1)S(1)} %bitcast.44, bf16[1024,1024]{1,0:T(8,128)(2,1)} %all-gather.6.cloned.1.call-done), kind=kOutput, calls=%fused_computation.50 | convolution fusion | flops 2147483648 | bytes 8388608 | tf_op jit(solution)/shard_map/dot_general | solution.py:76
  278.7 35.2 %all-gather.8.cloned.1.call-done = bf16[1024,1024]{1,0:T(8,128)(2,1)} async-done(((bf16[128,1024]{1,0:T(8,128)(2,1)}), bf16[1024,1024]{1,0:T(8,128)(2,1)}) %all-gather.8.cloned.1.call-update) | async-done | bytes 2097168 | tf_op jit(solution)/shard_map/all_gather | solution.py:72
  313.8 7.2 %add_convert_fusion = bf16[1024,1024]{1,0:T(8,128)(2,1)} fusion(f32[1024,1024]{1,0:T(8,128)} %fusion.23, bf16[1024,1024]{1,0:T(8,128)(2,1)} %bitcast.46, bf16[1024,1024]{1,0:T(8,128)(2,1)} %all-gather.8.cloned.1.call-done), kind=kOutput, calls=%fused_computation.7 | convolution fusion | flops 2149580800 | bytes 10485760 | tf_op jit(solution)/shard_map/dot_general | solution.py:76
  321.0 7.2 %all-to-all-start.2 = ((bf16[32,32,1024]{2,1,0:T(8,128)(2,1)}), bf16[32,32,1024]{2,1,0:T(8,128)(2,1)}, u32[]{:S(2)}, u32[]{:S(2)}) async-start(bf16[32,32,1024]{2,1,0:T(8,128)(2,1)} %bitcast.10), calls=%async_computation.4 | async-start | bytes 4194304 | tf_op jit(solution)/shard_map/all_to_all | solution.py:81
  328.3 0.0 copy-start.1
  328.3 2.2 multiply_reduce_fusion
  330.5 0.5 multiply_reduce_fusion.1
  331.0 82.5 %all-gather.1 = f32[32768]{0:T(1024)S(1)} all-gather(f32[1024]{0:T(1024)S(1)} %add.169), channel_id=3, replica_groups=mesh['z_lo'=4,'core'=2,'z_hi'=2,'x'=4,'y'=4] {'core','x','y'}, dimensions={0}, use_global_device_ids=true | all-gather | bytes 135168 | tf_op jit(solution)/shard_map/all_gather | solution.py:79
  413.6 0.0 all-to-all-done.2
  413.6 2.0 convert_reduce_fusion
  415.6 0.7 broadcast_multiply_fusion
  (29 shorter events, 0.2 us)
Async XLA Ops:
  6.5 32.7 %copy-start = (bf16[4,64,4096]{2,1,0:T(8,128)(2,1)S(1)}, bf16[4,64,4096]{2,1,0:T(8,128)(2,1)}, u32[]{:S(2)}) copy-start(bf16[4,64,4096]{2,1,0:T(8,128)(2,1)} %param.7) | copy-start | bytes 6291460
  6.5 2.6 copy-start.5
  6.5 2.6 copy-start.8
  6.5 2.6 copy-start.9
  6.5 133.7 %all-gather.10.cloned.1.call-start = ((), (), s32[]{:S(2)}) async-start(), calls=%async_computation.9 | async-start | bytes 3145728 | tf_op jit(solution)/shard_map/all_gather | solution.py:43
  9.0 178.1 %reduce-scatter.3.cloned.1.call-start = ((), (), s32[]{:S(2)}) async-start(), calls=%async_computation.5 | async-start | bytes 2359296 | tf_op jit(solution)/shard_map/reduce_scatter | solution.py:71
  15.9 22.7 %copy-start.6 = (bf16[64,64]{1,0:T(8,128)(2,1)S(1)}, bf16[64,64]{1,0:T(8,128)(2,1)}, u32[]{:S(2)}) copy-start(bf16[64,64]{1,0:T(8,128)(2,1)} %constant.64) | copy-start | bytes 24580
  146.2 85.0 %reduce-scatter.5.cloned.1.call-start = ((), (), s32[]{:S(2)}) async-start(), calls=%async_computation.7 | async-start | bytes 2359296 | tf_op jit(solution)/shard_map/reduce_scatter | solution.py:71
  146.3 33.4 %copy-start.7 = (bf16[1,1024,1024]{2,1,0:T(8,128)(2,1)S(1)}, bf16[1,1024,1024]{2,1,0:T(8,128)(2,1)}, u32[]{:S(2)}) copy-start(bf16[1,1024,1024]{2,1,0:T(8,128)(2,1)} %all-gather.10.cloned.1.call-done) | copy-start | bytes 6291460
  178.4 1.3 copy-start.3
  183.5 89.3 %copy-start.2 = (bf16[32,32,1024]{2,1,0:T(8,128)(2,1)S(1)}, bf16[32,32,1024]{2,1,0:T(8,128)(2,1)}, u32[]{:S(2)}) copy-start(bf16[32,32,1024]{2,1,0:T(8,128)(2,1)} %all_to_all.15) | copy-start | bytes 6291460
  183.5 89.2 %all-gather.6.cloned.1.call-start = ((), (), s32[]{:S(2)}) async-start(), calls=%async_computation.6 | async-start | bytes 2359296 | tf_op jit(solution)/shard_map/all_gather | solution.py:72
  187.1 126.7 %all-gather.8.cloned.1.call-start = ((), (), s32[]{:S(2)}) async-start(), calls=%async_computation.8 | async-start | bytes 2359296 | tf_op jit(solution)/shard_map/all_gather | solution.py:72
  321.0 92.6 %all-to-all-start.2 = ((bf16[32,32,1024]{2,1,0:T(8,128)(2,1)}), bf16[32,32,1024]{2,1,0:T(8,128)(2,1)}, u32[]{:S(2)}, u32[]{:S(2)}) async-start(bf16[32,32,1024]{2,1,0:T(8,128)(2,1)} %bitcast.10), calls=%async_computation.4 | async-start | bytes 4194304 | tf_op jit(solution)/shard_map/all_to_all | solution.py:81
  328.2 2.2 copy-start.4
  328.3 88.0 %copy-start.1 = (bf16[4,64,4096]{2,1,0:T(8,128)(2,1)S(1)}, bf16[4,64,4096]{2,1,0:T(8,128)(2,1)}, u32[]{:S(2)}) copy-start(bf16[4,64,4096]{2,1,0:T(8,128)(2,1)} %param.7) | copy-start | bytes 6291460
Sparse Core Ops, SparseCore 0:
  9.1 18.5 all-gather.9
  146.4 40.6 reduce-scatter.2
  189.6 41.5 reduce-scatter.4
  232.9 39.8 all-gather.5
  274.4 39.4 all-gather.7

commit v2 on v1

v2 whole, which is shorter than its diff:
```python
import math

import jax
import jax.numpy as jnp
import numpy as np
from jax import lax
from jax.experimental import pallas as pl
from jax.experimental.pallas import tpu as pltpu
from jax.sharding import Mesh, PartitionSpec as P

GRID = 64
KYZ = 32
box_length = 10.0
screening = 1.0
epsilon = 1e-06
PLANE = ("core", "x", "y")
RING = ("z_hi", "z_lo")
BLOCK = 8
YGRP = 8
HALF = 16
f32 = jnp.float32
bf16 = jnp.bfloat16


def real_basis(points, mode_count):
    cell = np.arange(points, dtype=np.float32)[:, None]
    mode = np.arange(mode_count, dtype=np.int32)[None, :]
    freq = (mode + 1) // 2
    phases = 2.0 * math.pi * cell * freq.astype(np.float32) / points
    values = np.where((mode % 2 == 1) | (mode == 0), np.cos(phases), np.sin(phases))
    factor = np.where((mode == 0) | (2 * freq == points), math.sqrt(1.0 / points), math.sqrt(2.0 / points))
    return (values * factor).astype(np.float32)


def constants():
    basis_x = real_basis(GRID, GRID)
    basis_p = real_basis(GRID, KYZ)
    eye_y = np.eye(YGRP, dtype=np.float32)
    eye_k = np.eye(HALF, dtype=np.float32)
    eye_p = np.eye(BLOCK, dtype=np.float32)
    split = basis_p.reshape(GRID, 2, HALF)
    along_z = np.einsum("yw,zqk->yzqwk", eye_y, split).reshape(YGRP * GRID, YGRP * KYZ)
    along_y = np.einsum("yb,km->ykbm", basis_p, eye_k).reshape(GRID * HALF, KYZ * HALF)
    along_x = np.einsum("xk,pr->kprx", basis_x, eye_p).reshape(GRID * BLOCK, BLOCK * GRID)
    freq_x = ((np.arange(GRID) + 1) // 2).astype(np.float32)
    freq_p = ((np.arange(KYZ) + 1) // 2).astype(np.float32)
    freq_q = freq_p.reshape(2, HALF)
    square = (
        (freq_x**2)[:, None, None, None]
        + (freq_p**2)[None, None, :, None]
        + (freq_q**2)[None, :, None, :]
    ).astype(np.float32)
    wave = np.float32((2.0 * math.pi / box_length) ** 2) * square
    weight = np.sqrt(np.float32(4.0 * math.pi) / (wave + np.float32(screening * screening)))
    weight = weight.reshape(GRID, 1, KYZ * KYZ).astype(np.float32)
    return (
        jnp.asarray(along_z).astype(bf16),
        jnp.asarray(along_y).astype(bf16),
        jnp.asarray(along_x).astype(bf16),
        jnp.asarray(weight),
    )


def gamma_kernel(po, pv, occ, vir, along_z, along_y, along_x, weight, out, dens, first, second):
    step = pl.program_id(0)
    rows = BLOCK * GRID
    tile_in = YGRP * GRID
    tile_out = YGRP * HALF
    width = KYZ * HALF
    for r in range(BLOCK):
        o = po[step * BLOCK + r]
        v = pv[step * BLOCK + r]
        dens[r * GRID : (r + 1) * GRID, :] = occ[o] * vir[v]
    for j in range(GRID // YGRP):
        t = jnp.dot(dens[:, j * tile_in : (j + 1) * tile_in], along_z[...], preferred_element_type=f32).astype(bf16)
        first[0, :, j * tile_out : (j + 1) * tile_out] = t[:, :tile_out]
        first[1, :, j * tile_out : (j + 1) * tile_out] = t[:, tile_out:]
    for q in range(2):
        second[:, q * width : (q + 1) * width] = jnp.dot(
            first[q], along_y[...], preferred_element_type=f32
        ).astype(bf16)
    piece = 256
    plane = KYZ * KYZ
    for n in range(plane // piece):
        g = jnp.dot(along_x[...], second[:, n * piece : (n + 1) * piece], preferred_element_type=f32)
        g = g.reshape(GRID, BLOCK, piece) * weight[:, :, n * piece : (n + 1) * piece]
        g = g.astype(bf16).reshape(GRID // 2, 2, BLOCK, piece)
        out[:, :, n * piece : (n + 1) * piece] = g[:, 0]
        out[:, :, plane + n * piece : plane + (n + 1) * piece] = g[:, 1]


def make_gamma(occ, vir, pair_occ, pair_vir):
    pairs = pair_occ.shape[0]
    along_z, along_y, along_x, weight = constants()
    rows = BLOCK * GRID
    full = lambda shape: pl.BlockSpec(shape, lambda i, a, b: (0,) * len(shape), pipeline_mode=pl.Buffered(1))
    return pl.pallas_call(
        gamma_kernel,
        out_shape=jax.ShapeDtypeStruct((GRID // 2, pairs, 2 * KYZ * KYZ), bf16),
        grid_spec=pltpu.PrefetchScalarGridSpec(
            num_scalar_prefetch=2,
            grid=(pairs // BLOCK,),
            in_specs=[
                full(occ.shape),
                full(vir.shape),
                full(along_z.shape),
                full(along_y.shape),
                full(along_x.shape),
                full(weight.shape),
            ],
            out_specs=pl.BlockSpec((GRID // 2, BLOCK, 2 * KYZ * KYZ), lambda i, a, b: (0, i, 0)),
            scratch_shapes=[
                pltpu.VMEM((rows, GRID * GRID), bf16),
                pltpu.VMEM((2, rows, GRID * HALF), bf16),
                pltpu.VMEM((rows, KYZ * KYZ), bf16),
            ],
        ),
        cost_estimate=pl.CostEstimate(flops=11_000_000_000, bytes_accessed=14_000_000, transcendentals=0),
        name="gamma",
    )(pair_occ, pair_vir, occ, vir, along_z, along_y, along_x, weight)


def body(occ_orbitals, vir_orbitals, pair_occ, pair_vir, sketch):
    pairs = pair_occ.shape[0]
    fields = sketch.shape[1]
    coef_count = GRID * KYZ * KYZ
    mine = sketch.reshape(2, -1, fields)[lax.axis_index("z_hi")]
    sketch_plane = lax.all_gather(mine, "core", axis=0, tiled=True)

    gamma = make_gamma(occ_orbitals, vir_orbitals, pair_occ, pair_vir)
    got = lax.all_to_all(gamma, PLANE, split_axis=0, concat_axis=0, tiled=True)
    got = got.reshape(32 * pairs, -1)
    part = lax.dot_general(sketch_plane, got, (((0,), (0,)), ((), ())), preferred_element_type=f32)
    mine_sum = lax.psum_scatter(part.astype(bf16), RING, scatter_dimension=0, tiled=True)
    whole = lax.all_gather(mine_sum, RING, axis=0, tiled=True)
    squares = jnp.sum(jnp.square(mine_sum.astype(f32)), axis=1)
    spread = jnp.broadcast_to(squares[None, None, :], (32, 8, squares.shape[0]))
    squares = jnp.sum(lax.all_to_all(spread, PLANE, split_axis=0, concat_axis=0, tiled=True)[:, 0, :], axis=0)
    scale = lax.rsqrt(squares / coef_count + epsilon) * (1.0 / math.sqrt(coef_count))
    spread = jnp.broadcast_to(scale[None, None, :], (8, 8, squares.shape[0]))
    scale = lax.all_to_all(spread, RING, split_axis=0, concat_axis=0, tiled=True)[:, 0, :].reshape(1, fields)

    vertex = lax.dot_general(got, whole, (((1,), (1,)), ((), ())), preferred_element_type=f32).astype(bf16)
    shares = lax.all_to_all(vertex.reshape(32, pairs, fields), PLANE, split_axis=0, concat_axis=0, tiled=True)
    return jnp.sum(shares.astype(f32), axis=0) * scale


def solution(mesh):
    wide = Mesh(mesh.devices.reshape(4, 2, 2, 4, 4), ("z_lo", "core", "z_hi", "x", "y"))
    whole = ("z_lo", "core", "z_hi", "x", "y")
    return jax.shard_map(
        body,
        mesh=wide,
        in_specs=(P(whole), P(whole), P(whole), P(whole), P(("z_lo", "core"))),
        out_specs=P(whole),
        check_vma=False,
    )
```

time: 426 us -> 267 us (0.63)
  blocking collectives: 150 us -> 14.8 us
  waiting for transfers between devices: 124 us -> 174 us
  local copies, waits for them, and re-layouts: 44.3 us -> 1.71 us
  matrix products: 50.5 us -> 18.7 us
  other arithmetic: 32.5 us -> 3.89 us
  Pallas kernels: 0 us -> 16.8 us
  starting transfers between devices: 7.65 us -> 21.4 us
    all_gather x1 -> x0, blocking collectives: 82.5 us -> none  [body(): all_squares = lax.all_gather(squares[None], PLANE, axis=0, tiled=True)]
    all_to_all x2 -> x1, blocking collectives: 67.9 us -> 14.8 us  [body(): lax.all_to_all(spread, PLANE, split_axis=0, concat_axis=0, tiled=True)]
    all_gather x2 -> x1, waiting for transfers between devices: 76.7 us -> 32.6 us  [body(): whole = lax.all_gather(mine_sum, RING, axis=0, tiled=True)]
    all_to_all x0 -> x2, waiting for transfers between devices: none -> 36.1 us  [the longest x1 36.1 us: body(): got = lax.all_to_all(gamma, PLANE, split_axis=0, concat_axis=0, tiled=True)]
    dot_general x5 -> x1, matrix products: 40.7 us -> 9.35 us  [body(): lax.dot_general(got, whole, (((1,), (1,)), ((), ())), preferred_element_t...]
    all_to_all x1, waiting for transfers between devices: 0.01 us -> 29.3 us  [body(): lax.all_to_all(vertex.reshape(32, pairs, fields), PLANE, split_axis=0, co...]
    convert_element_type x1 -> x0, local copies, waits for them, and re-layouts: 22.7 us -> none  [body(): kron_yz = (basis_p.astype(f32)[:, None, :, None] * basis_p.astype(f32)[No...]
    all_gather x1, waiting for transfers between devices: 0.01 us -> 19.9 us  [body(): sketch_plane = lax.all_gather(mine, 'core', axis=0, tiled=True)]
  transfers between devices with their start and end apart: 6 -> 6, of which waited for: 4 -> 5; matrix products, arithmetic and copies ran while one was open for 25% -> 5% of each run, Pallas kernels for 0% -> 0%
where the time goes in v2:
time: 267 us; the launch traced here: 264 us
  waiting for transfers between devices  174 us (65%)
  starting transfers between devices  21.4 us (8%)
  matrix products  18.7 us (7%)
  Pallas kernels  16.8 us (6%)
  blocking collectives  14.8 us (6%)
  between operations  13.2 us (5%)
  other arithmetic  3.89 us (1%)
    reduce_scatter x1, waiting for transfers between devices, body(): lax.psum_scatter(part.astype(bf16), RING, scatter_dimension=0, tiled=True)  56 us
    all_to_all x1, waiting for transfers between devices, body(): got = lax.all_to_all(gamma, PLANE, split_axis=0, concat_axis=0, tiled=True)  36.1 us
    all_gather x1, waiting for transfers between devices, body(): whole = lax.all_gather(mine_sum, RING, axis=0, tiled=True)  32.6 us
    all_to_all x1, waiting for transfers between devices, body(): lax.all_to_all(vertex.reshape(32, pairs, fields), PLANE, split_axis=0, co...  29.3 us
    all_gather x1, waiting for transfers between devices, body(): sketch_plane = lax.all_gather(mine, 'core', axis=0, tiled=True)  19.9 us
    pallas_call x1, Pallas kernels, make_gamma(): pl.pallas_call(gamma_kernel, out_shape=jax.ShapeDtypeStruct((GRID // 2, p...  16.8 us
    all_to_all x1, blocking collectives, body(): lax.all_to_all(spread, PLANE, split_axis=0, concat_axis=0, tiled=True)  14.8 us
    dot_general x1, matrix products, body(): lax.dot_general(sketch_plane, got, (((0,), (0,)), ((), ())), preferred_el...  9.36 us
  transfers between devices with their start and end apart: 6, of which 5 were waited for; matrix products, arithmetic and copies ran while one was open for 5% of the time, Pallas kernels for 0%

profile of v2, /device:TPU:32, one launch (start us, length us, event | category | flops | bytes accessed | tf_op | source)
XLA Modules:
  0.0 264.5 jit_solution(5728335952057542570)
XLA Ops:
  6.5 0.0 copy-start
  6.5 16.8 %gamma.1 = bf16[32,32,2048]{2,1,0:T(8,128)(2,1)} custom-call(s32[32]{0:T(128)} %po.1, s32[32]{0:T(128)} %pv.1, bf16[4,64,4096]{2,1,0:T(8,128)(2,1)} %occ.1, bf16[8,64,4096]{2,1,0:T(8,128)(2,1)} %vir.1, bf16[512,256]{1,0:T(8,128)(2,1)} %constant.35.along_z, bf16[1024,512]{1,0:T(8,128)(2,1)} %constant.36.along_y, bf16[512,512]{1,0:T(8,128)(2,1)} %constant.37.along_x, ...), custom_call_target="tpu_custom_call" | custom-call | flops 11000000512 | bytes 14000000 | tf_op jit(solution)/shard_map/gamma/pallas_call | solution.py:97
  23.4 7.4 %all-to-all-start = ((bf16[32,32,2048]{2,1,0:T(8,128)(2,1)}), bf16[32,32,2048]{2,1,0:T(8,128)(2,1)}, u32[]{:S(2)}, u32[]{:S(2)}) async-start(bf16[32,32,2048]{2,1,0:T(8,128)(2,1)} %gamma.1), calls=%async_computation | async-start | bytes 8388608 | tf_op jit(solution)/shard_map/all_to_all | solution.py:131
  30.8 0.0 all-gather.6.cloned.1.call-start
  30.9 0.0 copy-done
  30.9 1.1 constant_dynamic-slice_fusion
  32.0 0.0 all-gather.6.cloned.1.call-update
  32.0 0.0 reduce-scatter.2.cloned.1.call-start
  32.0 19.9 %all-gather.6.cloned.1.call-done = bf16[1,1024,1024]{2,1,0:T(8,128)(2,1)} async-done(((bf16[1,512,1024]{2,1,0:T(8,128)(2,1)}), bf16[1,1024,1024]{2,1,0:T(8,128)(2,1)}) %all-gather.6.cloned.1.call-update) | async-done | bytes 2097168 | tf_op jit(solution)/shard_map/all_gather | solution.py:128
  52.0 36.1 %all-to-all-done = bf16[32,32,2048]{2,1,0:T(8,128)(2,1)} async-done(((bf16[32,32,2048]{2,1,0:T(8,128)(2,1)}), bf16[32,32,2048]{2,1,0:T(8,128)(2,1)}, u32[]{:S(2)}, u32[]{:S(2)}) %all-to-all-start) | async-done | bytes 4194336 | tf_op jit(solution)/shard_map/all_to_all | solution.py:131
  88.1 9.4 %convolution_convert_fusion = bf16[1024,2048]{1,0:T(8,128)(2,1)} fusion(bf16[1024,2048]{1,0:T(8,128)(2,1)} %bitcast, bf16[1,1024,1024]{2,1,0:T(8,128)(2,1)} %all-gather.6.cloned.1.call-done), kind=kOutput, calls=%fused_computation.1 | convolution fusion | flops 4297064448 | bytes 10485760 | tf_op jit(solution)/shard_map/dot_general | solution.py:133
  97.5 0.0 reduce-scatter.2.cloned.1.call-update
  97.5 0.0 all-gather.4.cloned.1.call-start
  97.5 56.0 %reduce-scatter.2.cloned.1.call-done = bf16[128,2048]{1,0:T(8,128)(2,1)} async-done(((bf16[1024,2048]{1,0:T(8,128)(2,1)}), bf16[128,2048]{1,0:T(8,128)(2,1)}) %reduce-scatter.2.cloned.1.call-update) | async-done | bytes 524304 | tf_op jit(solution)/shard_map/reduce_scatter | solution.py:134
  153.5 0.0 all-gather.4.cloned.1.call-update
  153.5 1.2 multiply_reduce_fusion
  154.8 14.8 %all_to_all.20 = f32[32,8,128]{2,1,0:T(8,128)S(1)} all-to-all(f32[32,8,128]{2,1,0:T(8,128)S(1)} %broadcast_in_dim.4), channel_id=1, replica_groups=mesh['z_lo'=4,'core'=2,'z_hi'=2,'x'=4,'y'=4] {'core','x','y'}, dimensions={0} | all-to-all | bytes 262144 | tf_op jit(solution)/shard_map/all_to_all | solution.py:138
  169.6 0.6 broadcast_in_dim.5
  170.3 6.6 %all-to-all-start.3 = ((f32[8,8,128]{2,1,0:T(8,128)}), f32[8,8,128]{2,1,0:T(8,128)S(1)}, u32[]{:S(2)}, u32[]{:S(2)}) async-start(f32[8,8,128]{2,1,0:T(8,128)} %broadcast_in_dim.5), calls=%async_computation.4 | async-start | bytes 65536 | tf_op jit(solution)/shard_map/all_to_all | solution.py:141
  176.8 32.6 %all-gather.4.cloned.1.call-done = bf16[1024,2048]{1,0:T(8,128)(2,1)} async-done(((bf16[128,2048]{1,0:T(8,128)(2,1)}), bf16[1024,2048]{1,0:T(8,128)(2,1)}) %all-gather.4.cloned.1.call-update) | async-done | bytes 4194320 | tf_op jit(solution)/shard_map/all_gather | solution.py:135
  209.4 9.3 %convolution_convert_fusion.1 = bf16[1024,1024]{1,0:T(8,128)(2,1)} fusion(bf16[1024,2048]{1,0:T(8,128)(2,1)} %bitcast, bf16[1024,2048]{1,0:T(8,128)(2,1)} %all-gather.4.cloned.1.call-done), kind=kOutput, calls=%fused_computation.3 | convolution fusion | flops 4296015872 | bytes 10485760 | tf_op jit(solution)/shard_map/dot_general | solution.py:143
  218.8 0.0 all-to-all-done.3
  218.8 7.2 %all-to-all-start.1 = ((bf16[32,32,1024]{2,1,0:T(8,128)(2,1)}), bf16[32,32,1024]{2,1,0:T(8,128)(2,1)}, u32[]{:S(2)}, u32[]{:S(2)}) async-start(bf16[32,32,1024]{2,1,0:T(8,128)(2,1)} %bitcast.12), calls=%async_computation.2 | async-start | bytes 4194304 | tf_op jit(solution)/shard_map/all_to_all | solution.py:144
  226.0 29.3 %all-to-all-done.1 = bf16[32,32,1024]{2,1,0:T(8,128)(2,1)} async-done(((bf16[32,32,1024]{2,1,0:T(8,128)(2,1)}), bf16[32,32,1024]{2,1,0:T(8,128)(2,1)}, u32[]{:S(2)}, u32[]{:S(2)}) %all-to-all-start.1) | async-done | bytes 2097184 | tf_op jit(solution)/shard_map/all_to_all | solution.py:144
  255.3 2.0 convert_reduce_fusion
  257.3 0.7 broadcast_multiply_fusion
  (5 shorter events, 0.1 us)
Async XLA Ops:
  6.5 24.4 %copy-start = (bf16[1024,1024]{1,0:T(8,128)(2,1)S(1)}, bf16[1024,1024]{1,0:T(8,128)(2,1)}, u32[]{:S(2)}) copy-start(bf16[1024,1024]{1,0:T(8,128)(2,1)} %param.13) | copy-start | bytes 6291460
  23.4 64.7 %all-to-all-start = ((bf16[32,32,2048]{2,1,0:T(8,128)(2,1)}), bf16[32,32,2048]{2,1,0:T(8,128)(2,1)}, u32[]{:S(2)}, u32[]{:S(2)}) async-start(bf16[32,32,2048]{2,1,0:T(8,128)(2,1)} %gamma.1), calls=%async_computation | async-start | bytes 8388608 | tf_op jit(solution)/shard_map/all_to_all | solution.py:131
  30.8 21.1 %all-gather.6.cloned.1.call-start = ((), (), s32[]{:S(2)}) async-start(), calls=%async_computation.7 | async-start | bytes 3145728 | tf_op jit(solution)/shard_map/all_gather | solution.py:128
  32.0 121.5 %reduce-scatter.2.cloned.1.call-start = ((), (), s32[]{:S(2)}) async-start(), calls=%async_computation.5 | async-start | bytes 4718592 | tf_op jit(solution)/shard_map/reduce_scatter | solution.py:134
  97.5 111.9 %all-gather.4.cloned.1.call-start = ((), (), s32[]{:S(2)}) async-start(), calls=%async_computation.6 | async-start | bytes 4718592 | tf_op jit(solution)/shard_map/all_gather | solution.py:135
  170.3 48.5 %all-to-all-start.3 = ((f32[8,8,128]{2,1,0:T(8,128)}), f32[8,8,128]{2,1,0:T(8,128)S(1)}, u32[]{:S(2)}, u32[]{:S(2)}) async-start(f32[8,8,128]{2,1,0:T(8,128)} %broadcast_in_dim.5), calls=%async_computation.4 | async-start | bytes 65536 | tf_op jit(solution)/shard_map/all_to_all | solution.py:141
  218.8 36.5 %all-to-all-start.1 = ((bf16[32,32,1024]{2,1,0:T(8,128)(2,1)}), bf16[32,32,1024]{2,1,0:T(8,128)(2,1)}, u32[]{:S(2)}, u32[]{:S(2)}) async-start(bf16[32,32,1024]{2,1,0:T(8,128)(2,1)} %bitcast.12), calls=%async_computation.2 | async-start | bytes 4194304 | tf_op jit(solution)/shard_map/all_to_all | solution.py:144
Sparse Core Ops, SparseCore 0:
  33.4 18.4 all-gather.5
  97.6 55.8 reduce-scatter.1
  155.3 54.0 all-gather.3
